TPU v7x, 256 devices: a whole 4x4x8 slice. The times are simulated.
256 devices in a mesh: band: 8 (over x_lo, y), dev: 32 (over x_hi, z, core).
Axes of the slice: x: 4 (x_hi: 2, x_lo: 2; x = x_hi * 2 + x_lo), y: 4, z: 8, core: 2. Of those that a mesh axis runs over, the one named last changes fastest.
Arguments:
- drive: float32 [2, 32, 131072], P(None, None, ('band', 'dev')), may hold values from -6 to 6
- coords: float32 [3, 131072], P(None, ('band', 'dev')), may hold values from 0 to 3
- rule_index: int32 [131072], P(('band', 'dev')), may hold values from 0 to 3
- rule_weight: float32 [4], replicated, may hold values from 0.1 to 0.4
- pair_cols: int32 [24576], P(('band', 'dev')), may hold values from 0 to 511, as said below
- pair_count: int32 [256], P(('band', 'dev')), may hold values from 12 to 96, as said below
Outputs:
- near_field: float32 [2, 32, 131072], P(None, None, ('band', 'dev'))
Inputs may be any that keep to these rules, and one draw needn't show every extreme that they name: `pair_cols`: for slot s of device k the listed block column lies from k * 2 + (s mod 2) up to that row plus 64 - 1; slots s < 2 list the diagonal pair. `pair_count`: some device has all 96 slots live.
All inputs are finite; a program needn't handle non-finite values.
Results may differ from a plain program's by a relative error of at most 0.0003.
Values sent between devices are 32-bit elements; how exact they have to be, the bound alone decides.
A program may use at most 64 MiB of HBM per device.

v0:
```python
import math

import jax
import jax.numpy as jnp
from jax import lax
from jax.experimental import pallas as pl
from jax.experimental.pallas import tpu as pltpu
from jax.sharding import PartitionSpec as P

BLOCK = 256
RULES = 4
SLOTS = 96
RINGS = 16
RING_LEN = 8
HOPS = 4
ROWS = 32
PACK = 72
WAVES = 25.0 / (2.0 * math.pi)
GAIN = 25.0 / (8.0 * math.pi**2)
SMOOTH = (0.05 * WAVES) ** 2
SINE = (2.6417539924711972, -1.0863767471480779, 0.1340056362838771, -0.007739908243745813)
FULL = 2.0 * math.sqrt(2.0)
HALF = math.sqrt(2.0)

VM = pl.BlockSpec(memory_space=pltpu.VMEM)
HBM = pl.BlockSpec(memory_space=pltpu.HBM)
MESH = pl.DeviceIdType.MESH
NT = (((1,), (1,)), ((), ()))
NN = (((1,), (0,)), ((), ()))


def place():
    me = lax.axis_index("band") * 32 + lax.axis_index("dev")
    return me // 16, (me // 2) % 8, me % 2


def device(ring, z, core):
    k = (ring % RINGS) * 16 + (z % RING_LEN) * 2 + core
    return (k // 32, k % 32)


def remote(src, dst, ssem, rsem, target):
    return pltpu.make_async_remote_copy(
        src_ref=src, dst_ref=dst, send_sem=ssem, recv_sem=rsem, device_id=target, device_id_type=MESH
    )


def partners(ring, z, core):
    peers = [device(ring, z + 1, core), device(ring, z - 1, core), device(ring, z, 1 - core)]
    for d in (1, -1, 2, -2):
        for c in range(2):
            peers.append(device(ring + d, z, c))
    return peers


def split(v):
    hi = v.astype(jnp.bfloat16)
    return hi, (v - hi.astype(jnp.float32)).astype(jnp.bfloat16)


def fill_vectors(src, slot, l_ref):
    for h in range(2):
        hi, lo = split(src[0:64, h * BLOCK:(h + 1) * BLOCK])
        k = 2 * slot + h
        l_ref[k, 0:64, 0:BLOCK] = hi
        l_ref[k, 64:128, 0:BLOCK] = lo
        l_ref[k, 0:32, BLOCK:] = -hi[32:]
        l_ref[k, 32:64, BLOCK:] = hi[:32]
        l_ref[k, 64:96, BLOCK:] = -lo[32:]
        l_ref[k, 96:128, BLOCK:] = lo[:32]


def far(way, ch):
    return ch // (NCH // 2) == way


CUTS = (0, 40, 72)
NCH = len(CUTS) - 1


def gather_kernel(x_hbm, c_hbm, rule_hbm, rw_hbm, cols_hbm, count_ref,
                  li_ref, lj_ref, p_ref, q_ref, table_ref, other_ref, w_ref,
                  b_ref, bi_ref, bj_ref, x_ref, c_ref, rule_ref, cols_ref, rw_ref,
                  seen_ref, ring_send, ring_recv, side_send, side_recv, load_sem, seen_sem):
    ring, z, core = place()
    loads = [pltpu.make_async_copy(src, dst, load_sem.at[n]) for n, (src, dst) in enumerate((
        (rule_hbm, rule_ref), (rw_hbm, rw_ref), (x_hbm, x_ref), (c_hbm, c_ref), (cols_hbm, cols_ref)))]
    for cp in loads:
        cp.start()
    barrier = pltpu.get_barrier_semaphore()
    peers = partners(ring, z, core)
    for peer in peers:
        pl.semaphore_signal(barrier, inc=1, device_id=peer, device_id_type=MESH)

    for cp in loads:
        cp.wait()
    rule = rule_ref[...]
    w = jnp.zeros((1, 512), jnp.float32)
    for r in range(RULES):
        w = jnp.where(rule == r, rw_ref[r], w)
    w_ref[...] = jnp.broadcast_to(w, (8, 512))
    b_ref[0:64, :] = x_ref[...] * (w * GAIN)
    b_ref[64:67, :] = c_ref[...] * WAVES
    b_ref[67:72, :] = jnp.full((5, 512), -2.0, jnp.float32)
    slot = lax.broadcasted_iota(jnp.int32, (1, SLOTS), 1)
    b_ref[67:68, 0:SLOTS] = jnp.where(slot < count_ref[0], cols_ref[...], -2).astype(jnp.float32)
    table_ref[...] = jnp.zeros_like(table_ref)

    pl.semaphore_wait(barrier, len(peers))
    started = []

    def launch(cp):
        cp.start()
        started.append(cp)

    def owner_of(way, h):
        return (z - (1 - 2 * way) * h) % RING_LEN

    def hop(way, h, ch):
        owner = owner_of(way, h)
        rows = pl.ds(CUTS[ch], CUTS[ch + 1] - CUTS[ch])
        src = b_ref.at[rows] if h == 0 else bi_ref.at[owner, rows]
        return remote(src, bi_ref.at[owner, rows], ring_send.at[way, h, ch], ring_recv.at[way, h, ch],
                      device(ring, z + 1 - 2 * way, core))

    for ch in range(NCH):
        for way in range(2):
            launch(hop(way, 0, ch))
    for n, (d, c) in enumerate(((1, 0), (1, 1), (2, 0), (2, 1))):
        launch(remote(b_ref, bj_ref.at[d * 2 + core], side_send.at[n],
                      side_recv.at[d * 2 + core], device(ring - d, z, c)))
    launch(remote(b_ref, bj_ref.at[core], side_send.at[4], side_recv.at[core],
                  device(ring, z, 1 - core)))

    lane = lax.broadcasted_iota(jnp.int32, (16, 128), 1)
    col = lax.broadcasted_iota(jnp.int32, (16, 128), 0)
    want = jnp.where(col < 12, (ring + col // 4) * 32 + z * 4 + col % 4, -1).astype(jnp.float32)

    def expand_i(src, k, listed=True):
        fill_vectors(src, k, li_ref)
        t = src[64:72, :].T
        for h in range(2):
            for d in range(3):
                p_ref[2 * k + h, d] = jnp.broadcast_to(t[h * BLOCK:(h + 1) * BLOCK, d:d + 1], (BLOCK, 128))
        if not listed:
            return
        hit = jnp.where(jnp.broadcast_to(src[67:68, 0:128], (16, 128)) == want, 1.0, 0.0)
        for i in range(2):
            m = jnp.sum(jnp.where(lane % 2 == i, hit, 0.0), axis=1, keepdims=True)
            table_ref[...] += jnp.where(lane == 2 * k + i, m, 0.0).astype(jnp.int32)

    def expand_j(src, k):
        fill_vectors(src, k, lj_ref)
        for h in range(2):
            q_ref[2 * k + h] = src[64:72, h * BLOCK:(h + 1) * BLOCK]

    expand_i(b_ref, z)
    expand_j(b_ref, core)
    for h in range(1, HOPS):
        for ch in range(NCH):
            for way in range(2):
                hop(way, h - 1, ch).wait_recv()
                if h < HOPS - 1 or far(way, ch):
                    launch(hop(way, h, ch))
        for way in range(2):
            k = owner_of(way, h)
            expand_i(bi_ref.at[k], k)
        js = ((1 - core, 4),) if h == 1 else ((4, 0), (5, 0)) if h == 2 else ((2, 0), (3, 0))
        for k, n in js:
            remote(b_ref, bj_ref.at[k], side_send.at[n], side_recv.at[k],
                   device(ring, z, 1 - core)).wait_recv()
            expand_j(bj_ref.at[k], k)
            if n == 4:
                expand_i(bj_ref.at[k], RING_LEN, listed=False)
        if h == HOPS - 1:
            have = table_ref[...]
            tally = jnp.sum(jnp.where(have > 0, 1.0, 0.0)).astype(jnp.int32)
            have = jnp.where(col == 15, tally, have)
            seen_ref[...] = have
            table_ref[...] = have
    note = remote(seen_ref, other_ref, seen_sem.at[0], seen_sem.at[1], device(ring, z, 1 - core))
    note.start()
    for way in range(2):
        for ch in range(NCH):
            if far(way, ch):
                hop(way, HOPS - 1, ch).wait_recv()
    k = (z + HOPS) % RING_LEN
    expand_i(bi_ref.at[k], k)
    note.wait()
    for cp in started:
        cp.wait_send()


def gather(x, coords, rule, rw, cols, count):
    f = jnp.float32
    b = jnp.bfloat16
    dma = pltpu.SemaphoreType.DMA
    s = jax.ShapeDtypeStruct
    return pl.pallas_call(
        gather_kernel,
        out_shape=(s((18, 128, 512), b), s((12, 128, 512), b), s((18, 3, 256, 128), f), s((12, 8, 256), f),
                   s((16, 128), jnp.int32), s((16, 128), jnp.int32), s((8, 512), f)),
        in_specs=[HBM] * 5 + [pl.BlockSpec(memory_space=pltpu.SMEM)],
        out_specs=(VM,) * 7,
        scratch_shapes=[pltpu.VMEM((PACK, 512), f), pltpu.VMEM((8, PACK, 512), f), pltpu.VMEM((6, PACK, 512), f),
                        pltpu.VMEM((64, 512), f), pltpu.VMEM((3, 512), f), pltpu.VMEM((1, 512), jnp.int32),
                        pltpu.VMEM((1, SLOTS), jnp.int32), pltpu.SMEM((RULES,), f), pltpu.VMEM((16, 128), jnp.int32),
                        dma((2, HOPS, NCH)), dma((2, HOPS, NCH)), dma((5,)), dma((6,)), dma((5,)), dma((2,))],
        compiler_params=pltpu.CompilerParams(collective_id=0, has_side_effects=True, vmem_limit_bytes=20 << 20),
    )(x, coords, rule, rw, cols, count)


def build_tile(row, col, p_ref, q_ref, hi_ref, lo_ref):
    qx = q_ref[col, 0:1, :]
    qy = q_ref[col, 1:2, :]
    qz = q_ref[col, 2:3, :]
    for r in range(0, BLOCK, ROWS):
        px = p_ref[row, 0, r:r + ROWS, :]
        py = p_ref[row, 1, r:r + ROWS, :]
        pz = p_ref[row, 2, r:r + ROWS, :]
        dx = jnp.concatenate([px, px], axis=1) - qx
        dy = jnp.concatenate([py, py], axis=1) - qy
        dz = jnp.concatenate([pz, pz], axis=1) - qz
        square = dx * dx + (dy * dy + (dz * dz + SMOOTH))
        inv = lax.rsqrt(square)
        turns = square * inv
        f = turns - jnp.round(turns)
        f2 = f * f
        poly = SINE[-1]
        for k in SINE[-2::-1]:
            poly = poly * f2 + k
        s = f * poly
        ss = s * s
        rest = FULL - ss
        sh = s * (rest * lax.rsqrt(rest))
        ch = HALF - ss
        t = inv * sh
        rh, rl = split(inv - t * sh)
        ih, il = split(t * ch)
        hi_ref[r:r + ROWS, 0:BLOCK] = rh
        hi_ref[r:r + ROWS, BLOCK:] = ih
        lo_ref[r:r + ROWS, 0:BLOCK] = rl
        lo_ref[r:r + ROWS, BLOCK:] = il


def dotf(a, b, dims):
    return lax.dot_general(a, b, dims, preferred_element_type=jnp.float32)


def apply_tile(row, col, md, mm, li_ref, lj_ref, hi_ref, lo_ref, yi_ref, yj_ref):
    a = dotf(lj_ref[col], hi_ref[...], NT)
    b = dotf(lj_ref[col, 0:64, :], lo_ref[...], NT)
    yi_ref[row] += md * (a[:64] + a[64:] + b)
    a = dotf(li_ref[row, :, 0:BLOCK], hi_ref[:, 0:BLOCK], NN) + dotf(li_ref[row, :, BLOCK:], hi_ref[:, BLOCK:], NN)
    b = dotf(li_ref[row, 0:64, 0:BLOCK], lo_ref[:, 0:BLOCK], NN) + dotf(
        li_ref[row, 0:64, BLOCK:], lo_ref[:, BLOCK:], NN)
    yj_ref[col] += mm * (a[:64] + a[64:] + b)


def compute_kernel(li, lj, p, q, table, other, yi_ref, yj_ref, counts, theirs, work, hi0, lo0, hi1, lo1, sem):
    _, z, core = place()
    loads = [pltpu.make_async_copy(table, counts, sem.at[0]), pltpu.make_async_copy(other, theirs, sem.at[1])]
    for cp in loads:
        cp.start()
    yi_ref[...] = jnp.zeros_like(yi_ref)
    yj_ref[...] = jnp.zeros_like(yj_ref)
    build_tile(2 * z, 2 * core, p, q, hi0, lo0)
    for cp in loads:
        cp.wait()

    gap = counts[15, 0] - theirs[15, 0]
    give = jnp.where(gap > 0, lax.shift_right_logical(gap, 1), 0)
    take = jnp.where(gap < 0, lax.shift_right_logical(-gap, 1), 0)

    def scan_own(ref, first, label, keep):
        def inner(n, passed):
            for i in range(2):
                for j in range(12):
                    m = ref[j, first + i]
                    work[n] = (label + i) * 4096 + j * 256 + m
                    live = m > 0
                    n = n + jnp.where(jnp.logical_and(live, keep(passed)), 1, 0)
                    passed = passed + jnp.where(live, 1, 0)
            return n
        return inner

    n = scan_own(counts, 2 * z, 2 * z, lambda k: jnp.logical_or(k == 0, k > give))(jnp.int32(0), jnp.int32(0))
    n = scan_own(theirs, 2 * z, 2 * RING_LEN, lambda k: jnp.logical_and(k > 0, k <= take))(n, jnp.int32(0))

    def scan_row(k, n):
        row = (2 * z + k) % (2 * RING_LEN)
        base = jnp.where(row > 2 * z, 4, 0)
        for j in range(8):
            m = counts[base + j, row]
            work[n] = row * 4096 + (base + j) * 256 + m
            n = n + jnp.where(m > 0, 1, 0)
        return n

    n = lax.fori_loop(2, 2 * RING_LEN, scan_row, n)
    for e in range(3):
        work[n + e] = 0

    def unpack(t):
        w = work[t]
        row = lax.shift_right_logical(w, 12)
        col = lax.shift_right_logical(w, 8) & 15
        m = w & 255
        owner = jnp.where(lax.shift_right_logical(row, 1) == RING_LEN, 1 - core, core)
        local = jnp.logical_or(lax.shift_right_logical(row, 1) == z, row >= 2 * RING_LEN)
        same = jnp.logical_and(local, col == owner * 2 + (row & 1))
        return row, col, m.astype(jnp.float32), jnp.where(same, 0, m).astype(jnp.float32)


    @pl.loop(0, (n + 1) // 2)
    def _(k):
        r0, c0, d0, m0 = unpack(2 * k)
        r1, c1, d1, m1 = unpack(2 * k + 1)
        r2, c2, _, _ = unpack(2 * k + 2)
        build_tile(r1, c1, p, q, hi1, lo1)
        apply_tile(r0, c0, d0, m0, li, lj, hi0, lo0, yi_ref, yj_ref)
        build_tile(r2, c2, p, q, hi0, lo0)
        apply_tile(r1, c1, d1, m1, li, lj, hi1, lo1, yi_ref, yj_ref)

    for i in range(2):
        yj_ref[2 * (1 - core) + i] += yi_ref[2 * RING_LEN + i]


def compute(li, lj, p, q, table, other):
    f = jnp.float32
    b = jnp.bfloat16
    return pl.pallas_call(
        compute_kernel,
        out_shape=(jax.ShapeDtypeStruct((18, 64, 256), f), jax.ShapeDtypeStruct((12, 64, 256), f)),
        in_specs=[VM] * 6, out_specs=(VM, VM),
        scratch_shapes=[pltpu.SMEM((16, 128), jnp.int32), pltpu.SMEM((16, 128), jnp.int32),
                        pltpu.SMEM((256,), jnp.int32),
                        pltpu.VMEM((256, 512), b), pltpu.VMEM((256, 512), b),
                        pltpu.VMEM((256, 512), b), pltpu.VMEM((256, 512), b),
                        pltpu.SemaphoreType.DMA((2,))],
        compiler_params=pltpu.CompilerParams(vmem_limit_bytes=24 << 20),
    )(li, lj, p, q, table, other)


PARTS = 4
SPAN = 64 // PARTS


def near(way, ch):
    return ch // (PARTS // 2) == way


def reduce_kernel(yi_ref, yj_ref, w_ref, out_ref, flow, side, ring_send, ring_recv, side_send, side_recv):
    ring, z, core = place()
    barrier = pltpu.get_barrier_semaphore()
    peers = partners(ring, z, core)
    for peer in peers:
        pl.semaphore_signal(barrier, inc=1, device_id=peer, device_id_type=MESH)
    pl.semaphore_wait(barrier, len(peers))
    started = []

    def part(ref, first, ch):
        return ref.at[pl.ds(first, 2), pl.ds(SPAN * ch, SPAN)]

    def hop(way, h, ch, src):
        return remote(src, part(flow.at[way, h], 0, ch), ring_send.at[way, h, ch], ring_recv.at[way, h, ch],
                      device(ring, z + 1 - 2 * way, core))

    def target(way, h):
        return (z + (1 - 2 * way) * (HOPS - h)) % RING_LEN

    def launch(cp):
        cp.start()
        started.append(cp)

    for ch in range(PARTS):
        for way in range(2):
            if near(way, ch):
                launch(hop(way, 0, ch, part(yi_ref, 2 * target(way, 0), ch)))
    for ch in range(PARTS):
        for way in range(2):
            if not near(way, ch):
                launch(hop(way, 1, ch, part(yi_ref, 2 * target(way, 1), ch)))
    n = 0
    for d in (1, 2):
        for c in range(2):
            launch(remote(yj_ref.at[pl.ds((d * 2 + c) * 2, 2)], side.at[(d - 1) * 2 + core], side_send.at[n],
                          side_recv.at[(d - 1) * 2 + core], device(ring + d, z, c)))
            n += 1
    launch(remote(yj_ref.at[pl.ds((1 - core) * 2, 2)], side.at[4], side_send.at[4], side_recv.at[4],
                  device(ring, z, 1 - core)))
    for h in range(1, HOPS):
        for first in (False, True):
            for ch in range(PARTS):
                for way in range(2):
                    if near(way, ch) != first or (h == 1 and not first):
                        continue
                    here = part(flow.at[way, h - 1], 0, ch)
                    hop(way, h - 1, ch, here).wait_recv()
                    rows = slice(SPAN * ch, SPAN * ch + SPAN)
                    flow[way, h - 1, :, rows, :] += yi_ref[pl.ds(2 * target(way, h), 2), rows, :]
                    launch(hop(way, h, ch, here))
    for way in range(2):
        for ch in range(PARTS):
            hop(way, HOPS - 1, ch, part(flow.at[way, 0], 0, ch)).wait_recv()
    for s in range(5):
        remote(side.at[s], side.at[s], side_send.at[s], side_recv.at[s], device(ring, z, 1 - core)).wait_recv()
    for h in range(2):
        total = yi_ref[2 * z + h] + yj_ref[2 * core + h]
        total += side[0, h] + side[1, h] + (side[2, h] + side[3, h]) + side[4, h]
        total += flow[0, HOPS - 1, h] + flow[1, HOPS - 1, h]
        out_ref[:, h * BLOCK:(h + 1) * BLOCK] = total * w_ref[0:1, h * BLOCK:(h + 1) * BLOCK]
    for cp in started:
        cp.wait_send()


def reduce(yi, yj, w):
    f = jnp.float32
    dma = pltpu.SemaphoreType.DMA
    return pl.pallas_call(
        reduce_kernel,
        out_shape=jax.ShapeDtypeStruct((64, 512), f),
        in_specs=[VM] * 3, out_specs=VM,
        scratch_shapes=[pltpu.VMEM((2, HOPS, 2, 64, 256), f), pltpu.VMEM((5, 2, 64, 256), f),
                        dma((2, HOPS, PARTS)), dma((2, HOPS, PARTS)), dma((5,)), dma((5,))],
        compiler_params=pltpu.CompilerParams(collective_id=1, has_side_effects=True, vmem_limit_bytes=16 << 20),
    )(yi, yj, w)


def body(drive, coords, rule_index, rule_weight, pair_cols, pair_count):
    held = [pltpu.with_memory_space_constraint(v, pltpu.HBM) for v in (
        drive.reshape(64, 512), coords, rule_index.reshape(1, 512), rule_weight, pair_cols.reshape(1, SLOTS))]
    li, lj, p, q, table, other, w = gather(*held, pair_count)
    yi, yj = compute(li, lj, p, q, table, other)
    return reduce(yi, yj, w).reshape(2, 32, 512)


def solution(mesh):
    both = ("band", "dev")
    in_specs = (P(None, None, both), P(None, both), P(both), P(), P(both), P(both))
    return jax.shard_map(body, mesh=mesh, in_specs=in_specs, out_specs=P(None, None, both), check_vma=False)
```

profile of v0, /device:TPU:1, one launch (start us, length us, event | category | flops | bytes accessed | tf_op | source)
XLA Modules:
  0.0 71.4 jit_solution(8754883787579732919)
XLA Ops:
  0.7 27.4 %shard_map.64 = (bf16[18,128,512]{2,1,0:T(8,128)(2,1)S(1)}, bf16[12,128,512]{2,1,0:T(8,128)(2,1)S(1)}, f32[18,3,256,128]{3,2,1,0:T(8,128)S(1)}, f32[12,8,256]{2,...) custom-call(f32[64,512]{1,0:T(8,128)} %bitcast.5, f32[3,512]{1,0:T(4,128)} %c_hbm.1, ...), custom_call_target="tpu_custom_call" | custom-call | tf_op jit(solution)/shard_map/pallas_call | solution.py:199
  28.0 15.4 %shard_map.65 = (f32[18,64,256]{2,1,0:T(8,128)S(1)}, f32[12,64,256]{2,1,0:T(8,128)S(1)}) custom-call(bf16[18,128,512]{2,1,0:T(8,128)(2,1)S(1)} %get-tuple-element.14.li, bf16[12,128,512]{2,1,0:T(8,128)(2,1)S(1)} %get-tuple-element.15.lj, f32[18,3,256,128]{3,2,1,0:T(8,128)S(1)} %get-tuple-element.16.p, f32[12,8,256]{2,1,0:T(8,128)S(1)} %get-tuple-element.17.q, ...), custom_call_target="tpu_custom_call" | custom-call | tf_op jit(solution)/shard_map/pallas_call | solution.py:331
  43.5 27.2 %shard_map.66 = f32[64,512]{1,0:T(8,128)S(1)} custom-call(f32[18,64,256]{2,1,0:T(8,128)S(1)} %get-tuple-element.20.yi_ref, f32[12,64,256]{2,1,0:T(8,128)S(1)} %get-tuple-element.21.yj_ref, f32[8,512]{1,0:T(8,128)S(1)} %get-tuple-element.22.w_ref), custom_call_target="tpu_custom_call" | custom-call | tf_op jit(solution)/shard_map/pallas_call | solution.py:419
  70.7 0.7 copy.9
where the time goes:
time: 71 us; the launch traced here: 71.4 us
  Pallas kernels  70 us (99%)
    pallas_call x1, Pallas kernels, gather(): pl.pallas_call(gather_kernel, out_shape=(s((18, 128, 512), b), s((12, 128...  27.4 us
    pallas_call x1, Pallas kernels, reduce(): pl.pallas_call(reduce_kernel, out_shape=jax.ShapeDtypeStruct((64, 512), f...  27.2 us
    pallas_call x1, Pallas kernels, compute(): pl.pallas_call(compute_kernel, out_shape=(jax.ShapeDtypeStruct((18, 64, 2...  15.4 us

commit v1 on v0

--- a/solution.py
+++ b/solution.py
@@ -311,7 +311,7 @@
         return row, col, m.astype(jnp.float32), jnp.where(same, 0, m).astype(jnp.float32)
 
 
-    @pl.loop(0, (n + 1) // 2)
+    @pl.loop(0, n // 2)
     def _(k):
         r0, c0, d0, m0 = unpack(2 * k)
         r1, c1, d1, m1 = unpack(2 * k + 1)
@@ -320,6 +320,11 @@
         apply_tile(r0, c0, d0, m0, li, lj, hi0, lo0, yi_ref, yj_ref)
         build_tile(r2, c2, p, q, hi0, lo0)
         apply_tile(r1, c1, d1, m1, li, lj, hi1, lo1, yi_ref, yj_ref)
+
+    @pl.when(n % 2 == 1)
+    def _():
+        row, col, md, mm = unpack(n - 1)
+        apply_tile(row, col, md, mm, li, lj, hi0, lo0, yi_ref, yj_ref)
 
     for i in range(2):
         yj_ref[2 * (1 - core) + i] += yi_ref[2 * RING_LEN + i]

time: 71 us -> 70.2 us (0.989); the launches traced: 71.4 us -> 69.8 us
  Pallas kernels: 70 us -> 68.5 us
    pallas_call x1, Pallas kernels: 27.2 us -> 20.8 us  [reduce(): pl.pallas_call(reduce_kernel, out_shape=jax.ShapeDtypeStruct((64, 512), f...]
    pallas_call x1, Pallas kernels: 15.4 us -> 20.3 us  [compute(): pl.pallas_call(compute_kernel, out_shape=(jax.ShapeDtypeStruct((18, 64, 2...]
where the time goes in v1:
time: 70.2 us; the launch traced here: 69.8 us
  Pallas kernels  68.5 us (98%)
    pallas_call x1, Pallas kernels, gather(): pl.pallas_call(gather_kernel, out_shape=(s((18, 128, 512), b), s((12, 128...  27.4 us
    pallas_call x1, Pallas kernels, reduce(): pl.pallas_call(reduce_kernel, out_shape=jax.ShapeDtypeStruct((64, 512), f...  20.8 us
    pallas_call x1, Pallas kernels, compute(): pl.pallas_call(compute_kernel, out_shape=(jax.ShapeDtypeStruct((18, 64, 2...  20.3 us

profile of v1, /device:TPU:1, one launch (start us, length us, event | category | flops | bytes accessed | tf_op | source)
XLA Modules:
  0.0 69.8 jit_solution(11600742169422648494)
XLA Ops:
  0.7 27.4 %shard_map.64 = (bf16[18,128,512]{2,1,0:T(8,128)(2,1)S(1)}, bf16[12,128,512]{2,1,0:T(8,128)(2,1)S(1)}, f32[18,3,256,128]{3,2,1,0:T(8,128)S(1)}, f32[12,8,256]{2,...) custom-call(f32[64,512]{1,0:T(8,128)} %bitcast.5, f32[3,512]{1,0:T(4,128)} %c_hbm.1, ...), custom_call_target="tpu_custom_call" | custom-call | tf_op jit(solution)/shard_map/pallas_call | solution.py:199
  28.0 20.3 %shard_map.65 = (f32[18,64,256]{2,1,0:T(8,128)S(1)}, f32[12,64,256]{2,1,0:T(8,128)S(1)}) custom-call(bf16[18,128,512]{2,1,0:T(8,128)(2,1)S(1)} %get-tuple-element.14.li, bf16[12,128,512]{2,1,0:T(8,128)(2,1)S(1)} %get-tuple-element.15.lj, f32[18,3,256,128]{3,2,1,0:T(8,128)S(1)} %get-tuple-element.16.p, f32[12,8,256]{2,1,0:T(8,128)S(1)} %get-tuple-element.17.q, ...), custom_call_target="tpu_custom_call" | custom-call | tf_op jit(solution)/shard_map/pallas_call | solution.py:336
  48.4 20.8 %shard_map.66 = f32[64,512]{1,0:T(8,128)S(1)} custom-call(f32[18,64,256]{2,1,0:T(8,128)S(1)} %get-tuple-element.20.yi_ref, f32[12,64,256]{2,1,0:T(8,128)S(1)} %get-tuple-element.21.yj_ref, f32[8,512]{1,0:T(8,128)S(1)} %get-tuple-element.22.w_ref), custom_call_target="tpu_custom_call" | custom-call | tf_op jit(solution)/shard_map/pallas_call | solution.py:424
  69.2 0.7 copy.9
